TPU v7x, 32 devices: a whole 2x2x4 slice. The times are simulated.
32 devices in a mesh: seq: 16 (over z, y, core), head: 2 (over x).
Axes of the slice: x: 2, y: 2, z: 4, core: 2. Of those that a mesh axis runs over, the one named last changes fastest.
Arguments:
- tokens: bfloat16 [8192, 5120], P(('seq', 'head')), may hold values from -6 to 6
- w_qkv: bfloat16 [3, 5120, 640], P(None, None, 'head'), may hold values from -0.078125 to 0.078125
- scale_exp: int32 [3, 40, 2], P(None, None, 'head'), may hold values from -2 to 1
- gate_mask: int32 [8192, 2], P('seq', 'head'), may hold values 0 or 1
- rate: float32 [2], P('head'), may hold values from 0.00044194172 to 0.0022097088
- fast_gate: bfloat16 [2, 320, 640], P('head'), may hold values from -0.3125 to 0.3125
- fast_up: bfloat16 [2, 320, 640], P('head'), may hold values from -0.3125 to 0.3125
- fast_down: bfloat16 [2, 320, 640], P('head'), may hold values from -0.25 to 0.25
Outputs:
- answers: bfloat16 [8192, 640], P(('seq', 'head'))
All inputs are finite; a program needn't handle non-finite values. No bound on the sum of `gate_mask` on one device may be relied on, other than what follows from the above.
Results may differ from a plain program's by a relative error of at most 0.012.
Values may be sent and summed in bfloat16 or wider, within the bound.
A program may use at most 64 MiB of HBM per device.

v0:
```python
import jax
import jax.numpy as jnp
from jax import lax
from jax.sharding import PartitionSpec as P


def local_grads(keys, values, weight, old):
    gate = jnp.dot(keys, old[0], preferred_element_type=jnp.float32)
    upper = jnp.dot(keys, old[1], preferred_element_type=jnp.float32)
    sigma = jax.nn.sigmoid(gate)
    active = gate * sigma
    hidden = (active * upper).astype(jnp.bfloat16)
    weighted = (weight[:, None] * values.astype(jnp.float32)).astype(jnp.bfloat16)
    d_hidden = jnp.dot(weighted, old[2], preferred_element_type=jnp.float32)
    d_gate = (d_hidden * upper * sigma * (1.0 + gate * (1.0 - sigma))).astype(jnp.bfloat16)
    d_upper = (d_hidden * active).astype(jnp.bfloat16)
    dims = (((0,), (0,)), ((), ()))
    grad_gate = lax.dot_general(keys, d_gate, dims, preferred_element_type=jnp.float32)
    grad_upper = lax.dot_general(keys, d_upper, dims, preferred_element_type=jnp.float32)
    grad_down = lax.dot_general(weighted, hidden, dims, preferred_element_type=jnp.float32)
    return jnp.stack([grad_gate, grad_upper, grad_down])


def respond(query, renorm):
    gate = jnp.dot(query, renorm[0], preferred_element_type=jnp.float32)
    upper = jnp.dot(query, renorm[1], preferred_element_type=jnp.float32)
    hidden = (jax.nn.silu(gate) * upper).astype(jnp.bfloat16)
    output = lax.dot_general(
        hidden, renorm[2], (((1,), (1,)), ((), ())), preferred_element_type=jnp.float32
    )
    scaled = output * lax.rsqrt(jnp.mean(output * output, axis=-1, keepdims=True) + 1e-05)
    return scaled.astype(jnp.bfloat16)


def body(tokens, w_qkv, scale_exp, gate_mask, rate, fast_gate, fast_up, fast_down):
    factor = jnp.exp2(scale_exp.astype(jnp.float32))[:, :, 0]
    block_rows = w_qkv.shape[1] // factor.shape[1]
    factor = jnp.repeat(factor, block_rows, axis=1)[:, :, None].astype(jnp.bfloat16)
    weff = w_qkv * factor
    triple = jnp.einsum(
        "rd,cdh->rch",
        lax.all_gather(tokens, "head", axis=0, tiled=True),
        weff,
        preferred_element_type=jnp.float32,
    ).astype(jnp.bfloat16)
    query = triple[:, 0]
    keys = triple[:, 1]
    values = triple[:, 2]
    weight = rate[0] * gate_mask[:, 0].astype(jnp.float32)
    old = jnp.stack([fast_gate[0], fast_up[0], fast_down[0]])
    partial_grads = local_grads(keys, values, weight, old)
    old_f = old.astype(jnp.float32)
    old_norm = jnp.sqrt(jnp.sum(old_f * old_f, axis=1))
    total = lax.psum(partial_grads, "seq")
    fresh = old_f + total
    new_sq = jnp.sum(fresh * fresh, axis=1)
    renorm = (fresh * (old_norm / jnp.sqrt(new_sq + 1e-06))[:, None, :]).astype(jnp.bfloat16)
    answer = respond(query, renorm)
    return lax.all_to_all(answer, "head", split_axis=0, concat_axis=1, tiled=True)


def solution(mesh):
    in_specs = (
        P(("seq", "head"), None),
        P(None, None, "head"),
        P(None, None, "head"),
        P("seq", "head"),
        P("head"),
        P("head", None, None),
        P("head", None, None),
        P("head", None, None),
    )
    out_specs = P(("seq", "head"), None)
    return jax.shard_map(body, mesh=mesh, in_specs=in_specs, out_specs=out_specs, check_vma=False)
```

profile of v0, /device:TPU:0, one launch (start us, length us, event | category | flops | bytes accessed | tf_op | source)
XLA Modules:
  0.0 218.8 jit_solution(169645211959964053)
XLA Ops:
  6.5 0.0 copy-start.5
  6.5 0.0 copy-start.4
  6.5 0.0 all-gather.2.cloned.1.call-start
  6.5 0.7 all-gather.2.cloned.1.call-update
  7.3 0.0 all-reduce.2.cloned.1.call-start
  8.0 0.0 copy-done.5
  8.0 0.1 broadcast_bitcast_fusion
  8.1 0.0 copy-done.4
  8.1 72.0 %all-gather.2.cloned.1.call-done = bf16[512,5120]{1,0:T(8,128)(2,1)} async-done(((bf16[256,5120]{1,0:T(8,128)(2,1)}), bf16[512,5120]{1,0:T(8,128)(2,1)}) %all-gather.2.cloned.1.call-update) | async-done | bytes 5242896 | tf_op jit(solution)/shard_map/all_gather | solution.py:42
  80.2 0.0 copy-start.2
  80.2 9.5 %fusion.10 = bf16[512,3,320]{0,2,1:T(8,128)(2,1)S(1)} fusion(bf16[512,5120]{1,0:T(8,128)(2,1)} %all-gather.2.cloned.1.call-done, bf16[3,5120,320]{1,2,0:T(8,128)(2,1)} %param.9, bf16[3,5120]{1,0:T(4,128)(2,1)S(1)} %bitcast.82), kind=kOutput, calls=%fused_computation.12 | convolution fusion | flops 5038571520 | bytes 16087040 | tf_op jit(solution)/shard_map/rd,cdh->rch/dot_general | solution.py:40
  89.7 0.0 copy-done.2
  89.7 0.0 copy-start.1
  89.7 0.6 fusion.23
  90.3 0.4 copy-done.1
  90.7 0.6 fusion.25
  91.3 0.4 copy-done.3
  91.7 0.6 fusion.27
  92.3 0.6 convolution_bitcast_fusion.1
  92.9 0.8 convolution_bitcast_fusion.2
  93.7 0.6 convolution_bitcast_fusion
  94.3 1.6 pad_maximum_fusion
  95.9 0.0 all-reduce.2.cloned.1.call-update
  96.0 100.3 %all-reduce.2.cloned.1.call-done = f32[3,320,640]{2,1,0:T(8,128)} async-done(((f32[3,320,640]{2,1,0:T(8,128)}), f32[3,320,640]{2,1,0:T(8,128)}) %all-reduce.2.cloned.1.call-update) | async-done | bytes 2457616 | tf_op jit(solution)/shard_map/psum | solution.py:54
  196.2 2.4 %fusion.4 = (f32[3,640]{1,0:T(4,128)S(1)}, f32[3,640]{1,0:T(4,128)S(1)}) fusion(bf16[1,320,640]{2,1,0:T(8,128)(2,1)S(1)} %copy-done.3, bf16[1,320,640]{2,1,0:T(8,128)(2,1)S(1)} %copy-done.1, bf16[1,320,640]{2,1,0:T(8,128)(2,1)S(1)} %copy-done.2, f32[3,320,640]{2,1,0:T(8,128)} %all-reduce.2.cloned.1.call-done), kind=kLoop, calls=%fused_computation.6 | loop fusion | flops 4911360 | bytes 3701760 | tf_op jit(solution)/shard_map/reduce_sum | solution.py:53
  198.6 0.1 copy-done
  198.7 0.4 multiply_convert_fusion
  199.0 1.6 fusion.22
  200.7 2.3 %multiply_reduce_fusion.1 = (f32[512]{0:T(512)S(1)}, f32[512,320]{0,1:T(8,128)S(1)}) fusion(bf16[3,320,640]{2,1,0:T(8,128)(2,1)S(1)} %multiply_convert_fusion, f32[512,640]{1,0:T(8,128)} %fusion.22, bf16[512,3,320]{0,2,1:T(8,128)(2,1)S(1)} %fusion.10), kind=kOutput, calls=%fused_computation.30 | convolution fusion | flops 421723648 | bytes 3115008 | tf_op jit(solution)/shard_map/dot_general | solution.py:28
  203.0 0.1 multiply_convert_fusion.6
  203.1 7.9 %all_to_all.19 = bf16[2,256,320]{1,2,0:T(8,128)(2,1)S(1)} all-to-all(bf16[2,256,320]{1,2,0:T(8,128)(2,1)S(1)} %bitcast.79), channel_id=1, replica_groups=mesh['seq'=16,'head'=2] {'head'}, dimensions={0} | all-to-all | bytes 655360 | tf_op jit(solution)/shard_map/all_to_all | solution.py:59
  211.1 0.9 copy.11
  (9 shorter events, 0.1 us)
Async XLA Ops:
  6.5 1.4 copy-start.5
  6.5 1.6 copy-start.4
  6.5 73.6 %all-gather.2.cloned.1.call-start = ((), (), s32[]{:S(2)}) async-start(), calls=%async_computation.1 | async-start | bytes 7864320 | tf_op jit(solution)/shard_map/all_gather | solution.py:42
  7.3 189.0 %all-reduce.2.cloned.1.call-start = ((), (), s32[]{:S(2)}) async-start(), calls=%async_computation.2 | async-start | bytes 4915200 | tf_op jit(solution)/shard_map/psum | solution.py:54
  80.2 9.5 %copy-start.2 = (bf16[1,320,640]{2,1,0:T(8,128)(2,1)S(1)}, bf16[1,320,640]{2,1,0:T(8,128)(2,1)}, u32[]{:S(2)}) copy-start(bf16[1,320,640]{2,1,0:T(8,128)(2,1)} %param.13) | copy-start | bytes 1228804
  89.7 1.0 copy-start.1
  90.7 1.0 copy-start.3
  196.2 2.4 %copy-start = (f32[3,320,640]{2,1,0:T(8,128)S(1)}, f32[3,320,640]{2,1,0:T(8,128)}, u32[]{:S(2)}) copy-start(f32[3,320,640]{2,1,0:T(8,128)} %all-reduce.2.cloned.1.call-done) | copy-start | bytes 7372804
Sparse Core Ops, SparseCore 0:
  8.9 71.2 all-gather.1
  96.1 100.1 all-reduce.1
where the time goes:
time: 219 us
  waiting for transfers between devices  173 us (79%)
  matrix products  17.3 us (8%)
  between operations  14.2 us (6%)
  blocking collectives  7.95 us (4%)
  other arithmetic  4.41 us (2%)
    psum x1, waiting for transfers between devices, body(): total = lax.psum(partial_grads, 'seq')  100 us
    all_gather x1, waiting for transfers between devices, body(): lax.all_gather(tokens, 'head', axis=0, tiled=True)  72 us
    dot_general x1, matrix products, body(): jnp.einsum('rd,cdh->rch', lax.all_gather(tokens, 'head', axis=0, tiled=Tr...  9.51 us
    all_to_all x1, blocking collectives, body(): lax.all_to_all(answer, 'head', split_axis=0, concat_axis=1, tiled=True)  7.95 us
  transfers between devices with their start and end apart: 2, of which 2 were waited for; matrix products, arithmetic and copies ran while one was open for 0% of the time, Pallas kernels for 0%

commit v1 on v0

--- a/solution.py
+++ b/solution.py
@@ -51,7 +51,9 @@
     partial_grads = local_grads(keys, values, weight, old)
     old_f = old.astype(jnp.float32)
     old_norm = jnp.sqrt(jnp.sum(old_f * old_f, axis=1))
-    total = lax.psum(partial_grads, "seq")
+    total = partial_grads
+    for hop in (1, 2, 4, 8):
+        total = total + lax.ppermute(total, "seq", [(dev, dev ^ hop) for dev in range(16)])
     fresh = old_f + total
     new_sq = jnp.sum(fresh * fresh, axis=1)
     renorm = (fresh * (old_norm / jnp.sqrt(new_sq + 1e-06))[:, None, :]).astype(jnp.bfloat16)

time: 219 us -> 338 us (1.54)
  waiting for transfers between devices: 173 us -> 289 us
  starting transfers between devices: 0.04 us -> 5.66 us
    ppermute x0 -> x4, waiting for transfers between devices: none -> 216 us  [body(): lax.ppermute(total, 'seq', [(dev, dev ^ hop) for dev in range(16)])]
    psum x1 -> x0, waiting for transfers between devices: 100 us -> none  [body(): total = lax.psum(partial_grads, 'seq')]
    ppermute x0 -> x4, starting transfers between devices: none -> 5.66 us  [body(): lax.ppermute(total, 'seq', [(dev, dev ^ hop) for dev in range(16)])]
  transfers between devices with their start and end apart: 2 -> 5, of which waited for: 2 -> 5; matrix products, arithmetic and copies ran while one was open for 0% -> 0% of each run, Pallas kernels for 0% -> 0%
where the time goes in v1:
time: 338 us
  waiting for transfers between devices  289 us (86%)
  matrix products  15.8 us (5%)
  between operations  14.2 us (4%)
  blocking collectives  7.92 us (2%)
  starting transfers between devices  5.66 us (2%)
  other arithmetic  3.38 us (1%)
    ppermute x4, waiting for transfers between devices, body(): lax.ppermute(total, 'seq', [(dev, dev ^ hop) for dev in range(16)])  216 us
    all_gather x1, waiting for transfers between devices, body(): lax.all_gather(tokens, 'head', axis=0, tiled=True)  72.1 us
    dot_general x1, matrix products, body(): jnp.einsum('rd,cdh->rch', lax.all_gather(tokens, 'head', axis=0, tiled=Tr...  9.53 us
    all_to_all x1, blocking collectives, body(): lax.all_to_all(answer, 'head', split_axis=0, concat_axis=1, tiled=True)  7.92 us
  transfers between devices with their start and end apart: 5, of which 5 were waited for; matrix products, arithmetic and copies ran while one was open for 0% of the time, Pallas kernels for 0%

profile of v1, /device:TPU:0, one launch (start us, length us, event | category | flops | bytes accessed | tf_op | source)
XLA Modules:
  0.0 338.1 jit_solution(2090559753048728656)
XLA Ops:
  6.5 0.7 all-gather.2.cloned.1.call-update
  7.9 0.1 broadcast_bitcast_fusion
  8.1 72.1 %all-gather.2.cloned.1.call-done = bf16[512,5120]{1,0:T(8,128)(2,1)} async-done(((bf16[256,5120]{1,0:T(8,128)(2,1)}), bf16[512,5120]{1,0:T(8,128)(2,1)}) %all-gather.2.cloned.1.call-update) | async-done | bytes 5242896 | tf_op jit(solution)/shard_map/all_gather | solution.py:42
  80.2 9.5 %fusion.10 = bf16[512,3,320]{0,2,1:T(8,128)(2,1)S(1)} fusion(bf16[512,5120]{1,0:T(8,128)(2,1)} %all-gather.2.cloned.1.call-done, bf16[3,5120,320]{1,2,0:T(8,128)(2,1)} %param.9, bf16[3,5120]{1,0:T(4,128)(2,1)S(1)} %bitcast.82), kind=kOutput, calls=%fused_computation.12 | convolution fusion | flops 5038571520 | bytes 16087040 | tf_op jit(solution)/shard_map/rd,cdh->rch/dot_general | solution.py:40
  89.7 0.0 copy-start.1
  89.7 0.6 fusion.23
  90.3 0.4 copy-done.1
  90.7 0.6 fusion.25
  91.3 0.4 copy-done
  91.7 0.6 fusion.27
  92.3 0.6 convolution_bitcast_fusion.1
  92.9 0.8 convolution_bitcast_fusion.2
  93.7 0.6 convolution_bitcast_fusion
  94.4 0.2 pad_maximum_fusion
  94.5 0.1 collective-permute-start
  94.6 4.7 %collective-permute-done = f32[3,320,640]{2,1,0:T(8,128)S(1)} collective-permute-done((f32[3,320,640]{2,1,0:T(8,128)S(1)}, f32[3,320,640]{2,1,0:T(8,128)S(1)}, u32[]{:S(2)}, u32[]{:S(2)}) %collective-permute-start) | collective-permute-done | bytes 2457632 | tf_op jit(solution)/shard_map/ppermute | solution.py:56
  99.3 0.2 fusion.42
  99.5 1.6 collective-permute-start.1
  101.1 53.9 %collective-permute-done.1 = f32[3,320,640]{2,1,0:T(8,128)S(1)} collective-permute-done((f32[3,320,640]{2,1,0:T(8,128)S(1)}, f32[3,320,640]{2,1,0:T(8,128)S(1)}, u32[]{:S(2)}, u32[]{:S(2)}) %collective-permute-start.1) | collective-permute-done | bytes 2457632 | tf_op jit(solution)/shard_map/ppermute | solution.py:56
  155.0 0.3 fusion.43
  155.3 1.6 collective-permute-start.2
  156.9 53.1 %collective-permute-done.2 = f32[3,320,640]{2,1,0:T(8,128)S(1)} collective-permute-done((f32[3,320,640]{2,1,0:T(8,128)S(1)}, f32[3,320,640]{2,1,0:T(8,128)S(1)}, u32[]{:S(2)}, u32[]{:S(2)}) %collective-permute-start.2) | collective-permute-done | bytes 2457632 | tf_op jit(solution)/shard_map/ppermute | solution.py:56
  209.9 0.2 add.50
  210.2 2.5 collective-permute-start.3
  212.7 104.8 %collective-permute-done.3 = f32[3,320,640]{2,1,0:T(8,128)S(1)} collective-permute-done((f32[3,320,640]{2,1,0:T(8,128)S(1)}, f32[3,320,640]{2,1,0:T(8,128)S(1)}, u32[]{:S(2)}, u32[]{:S(2)}) %collective-permute-start.3) | collective-permute-done | bytes 2457632 | tf_op jit(solution)/shard_map/ppermute | solution.py:56
  317.5 0.6 fusion.4
  318.2 0.5 multiply_convert_fusion
  318.7 0.6 fusion.22
  319.3 1.9 multiply_reduce_fusion.1
  321.2 1.2 multiply_convert_fusion.6
  322.4 7.9 %all_to_all.19 = bf16[2,256,320]{1,2,0:T(8,128)(2,1)S(1)} all-to-all(bf16[2,256,320]{1,2,0:T(8,128)(2,1)S(1)} %bitcast.79), channel_id=1, replica_groups=mesh['seq'=16,'head'=2] {'head'}, dimensions={0} | all-to-all | bytes 655360 | tf_op jit(solution)/shard_map/all_to_all | solution.py:61
  330.3 0.9 copy.11
  (15 shorter events, 0.1 us)
Async XLA Ops:
  6.5 1.4 copy-start.4
  6.5 1.5 copy-start.3
  6.5 73.6 %all-gather.2.cloned.1.call-start = ((), (), s32[]{:S(2)}) async-start(), calls=%async_computation.1 | async-start | bytes 7864320 | tf_op jit(solution)/shard_map/all_gather | solution.py:42
  80.2 9.5 %copy-start.2 = (bf16[1,320,640]{2,1,0:T(8,128)(2,1)S(1)}, bf16[1,320,640]{2,1,0:T(8,128)(2,1)}, u32[]{:S(2)}) copy-start(bf16[1,320,640]{2,1,0:T(8,128)(2,1)} %param.13) | copy-start | bytes 1228804
  89.7 1.0 copy-start.1
  90.7 1.0 copy-start
  94.5 4.7 %collective-permute-start = (f32[3,320,640]{2,1,0:T(8,128)S(1)}, f32[3,320,640]{2,1,0:T(8,128)S(1)}, u32[]{:S(2)}, u32[]{:S(2)}) collective-permute-start(f32[3,320,640]{2,1,0:T(8,128)S(1)} %pad_maximum_fusion), channel_id=1, source_target_pairs={{0,2},{2,0},{4,6},{6,4},{8,10},{10,8},{12,14},{14,12},{16,18},{18,... | collective-permute-start | bytes 7372808 | tf_op jit(solution)/shard_map/ppermute | solution.py:56
  99.5 55.5 %collective-permute-start.1 = (f32[3,320,640]{2,1,0:T(8,128)S(1)}, f32[3,320,640]{2,1,0:T(8,128)S(1)}, u32[]{:S(2)}, u32[]{:S(2)}) collective-permute-start(f32[3,320,640]{2,1,0:T(8,128)S(1)} %fusion.42), channel_id=1, source_target_pairs={{0,4},{2,6},{4,0},{6,2},{8,12},{10,14},{12,8},{14,10},{16,20},{18,... | collective-permute-start | bytes 7372808 | tf_op jit(solution)/shard_map/ppermute | solution.py:56
  155.3 54.6 %collective-permute-start.2 = (f32[3,320,640]{2,1,0:T(8,128)S(1)}, f32[3,320,640]{2,1,0:T(8,128)S(1)}, u32[]{:S(2)}, u32[]{:S(2)}) collective-permute-start(f32[3,320,640]{2,1,0:T(8,128)S(1)} %fusion.43), channel_id=1, source_target_pairs={{0,8},{2,10},{4,12},{6,14},{8,0},{10,2},{12,4},{14,6},{16,24},{18,... | collective-permute-start | bytes 7372808 | tf_op jit(solution)/shard_map/ppermute | solution.py:56
  210.2 107.3 %collective-permute-start.3 = (f32[3,320,640]{2,1,0:T(8,128)S(1)}, f32[3,320,640]{2,1,0:T(8,128)S(1)}, u32[]{:S(2)}, u32[]{:S(2)}) collective-permute-start(f32[3,320,640]{2,1,0:T(8,128)S(1)} %add.50), channel_id=1, source_target_pairs={{0,16},{2,18},{4,20},{6,22},{8,24},{10,26},{12,28},{14,30},{16,0},... | collective-permute-start | bytes 7372808 | tf_op jit(solution)/shard_map/ppermute | solution.py:56
Sparse Core Ops, SparseCore 0:
  8.9 71.2 all-gather.1

commit v2 on v0

--- a/solution.py
+++ b/solution.py
@@ -2,6 +2,25 @@
 import jax.numpy as jnp
 from jax import lax
 from jax.sharding import PartitionSpec as P
+
+
+def laid_out(blocks, dim):
+    blocks = jnp.moveaxis(blocks, 0, dim)
+    dims = blocks.shape
+    return blocks.reshape(*dims[:dim], dims[dim] * dims[dim + 1], *dims[dim + 2 :])
+
+
+def on_each_block(array, axis, dim, work, out_dim):
+    size, index, rows = (lax.axis_size(axis), lax.axis_index(axis), array.shape[dim])
+    right = [(i, (i + 1) % size) for i in range(size)]
+    blocks = []
+    carried = array
+    for step in range(size):
+        coming = carried if step == size - 1 else lax.ppermute(carried, axis, right)
+        blocks.append(work(carried, (index - step) % size * rows))
+        carried = coming
+    blocks = jnp.stack(blocks)[(index - jnp.arange(size)) % size]
+    return laid_out(blocks, out_dim)
 
 
 def local_grads(keys, values, weight, old):
@@ -37,11 +56,14 @@
     block_rows = w_qkv.shape[1] // factor.shape[1]
     factor = jnp.repeat(factor, block_rows, axis=1)[:, :, None].astype(jnp.bfloat16)
     weff = w_qkv * factor
-    triple = jnp.einsum(
-        "rd,cdh->rch",
-        lax.all_gather(tokens, "head", axis=0, tiled=True),
-        weff,
-        preferred_element_type=jnp.float32,
+    triple = on_each_block(
+        tokens,
+        "head",
+        0,
+        lambda part, offset: jnp.einsum(
+            "rd,cdh->rch", part, weff, preferred_element_type=jnp.float32
+        ),
+        0,
     ).astype(jnp.bfloat16)
     query = triple[:, 0]
     keys = triple[:, 1]

time: 219 us -> 204 us (0.932)
  waiting for transfers between devices: 173 us -> 149 us
  starting transfers between devices: 0.04 us -> 2.97 us
  matrix products: 17.3 us -> 19.7 us
    all_gather x1 -> x0, waiting for transfers between devices: 72 us -> none  [body(): lax.all_gather(tokens, 'head', axis=0, tiled=True)]
    ppermute x0 -> x1, waiting for transfers between devices: none -> 47.5 us  [on_each_block(): coming = carried if step == size - 1 else lax.ppermute(carried, axis, right)]
    ppermute x0 -> x1, starting transfers between devices: none -> 2.97 us  [on_each_block(): coming = carried if step == size - 1 else lax.ppermute(carried, axis, right)]
    dot_general x1 -> x2, matrix products: 9.51 us -> 11.9 us  [body(): jnp.einsum('rd,cdh->rch', part, weff, preferred_element_type=jnp.float32)]
  transfers between devices with their start and end apart: 2 -> 2, of which waited for: 2 -> 2; matrix products, arithmetic and copies ran while one was open for 0% -> 4% of each run, Pallas kernels for 0% -> 0%
where the time goes in v2:
time: 204 us; the launch traced here: 203 us
  waiting for transfers between devices  149 us (73%)
  matrix products  19.7 us (10%)
  between operations  14.2 us (7%)
  blocking collectives  7.94 us (4%)
  other arithmetic  5.88 us (3%)
  local copies, waits for them, and re-layouts  3.09 us (2%)
  starting transfers between devices  2.97 us (1%)
    psum x1, waiting for transfers between devices, body(): total = lax.psum(partial_grads, 'seq')  102 us
    ppermute x1, waiting for transfers between devices, on_each_block(): coming = carried if step == size - 1 else lax.ppermute(carried, axis, right)  47.5 us
    dot_general x2, matrix products, body(): jnp.einsum('rd,cdh->rch', part, weff, preferred_element_type=jnp.float32)  11.9 us
    all_to_all x1, blocking collectives, body(): lax.all_to_all(answer, 'head', split_axis=0, concat_axis=1, tiled=True)  7.94 us
  transfers between devices with their start and end apart: 2, of which 2 were waited for; matrix products, arithmetic and copies ran while one was open for 4% of the time, Pallas kernels for 0%

profile of v2, /device:TPU:0, one launch (start us, length us, event | category | flops | bytes accessed | tf_op | source)
XLA Modules:
  0.0 203.2 jit_solution(18418702981810311576)
XLA Ops:
  6.5 3.0 %collective-permute-start = (bf16[256,5120]{1,0:T(8,128)(2,1)}, bf16[256,5120]{1,0:T(8,128)(2,1)}, u32[]{:S(2)}, u32[]{:S(2)}) collective-permute-start(bf16[256,5120]{1,0:T(8,128)(2,1)} %param.8), channel_id=1, source_target_pairs={{0,1},{1,0},{2,3},{3,2},{4,5},{5,4},{6,7},{7,6},{8,9},{9,8},{10,11... | collective-permute-start | bytes 7864328 | tf_op jit(solution)/shard_map/ppermute | solution.py:19
  10.2 0.7 exponential_convert_fusion
  10.9 0.1 broadcast_bitcast_fusion
  11.0 0.7 convert_multiply_fusion.2
  11.7 7.4 %fusion.10 = bf16[1,256,3,320]{1,3,2,0:T(8,128)(2,1)S(1)} fusion(bf16[256,5120]{1,0:T(8,128)(2,1)} %param.8, bf16[3,5120,320]{1,2,0:T(8,128)(2,1)} %param.9, bf16[3,5120]{1,0:T(4,128)(2,1)S(1)} %bitcast.106), kind=kOutput, calls=%fused_computation.18 | convolution fusion | flops 2521497600 | bytes 12974080 | tf_op jit(solution)/shard_map/rd,cdh->rch/dot_general | solution.py:63
  19.1 47.5 %collective-permute-done = bf16[256,5120]{1,0:T(8,128)(2,1)} collective-permute-done((bf16[256,5120]{1,0:T(8,128)(2,1)}, bf16[256,5120]{1,0:T(8,128)(2,1)}, u32[]{:S(2)}, u32[]{:S(2)}) %collective-permute-start) | collective-permute-done | bytes 2621472 | tf_op jit(solution)/shard_map/ppermute | solution.py:19
  66.7 4.5 %fusion.15 = bf16[1,256,3,320]{1,3,2,0:T(8,128)(2,1)S(1)} fusion(bf16[256,5120]{1,0:T(8,128)(2,1)} %collective-permute-done, bf16[3,5120,320]{1,2,0:T(8,128)(2,1)S(1)} %copy-done.4, bf16[3,5120]{1,0:T(4,128)(2,1)S(1)} %bitcast.107), kind=kOutput, calls=%fused_computation.19 | convolution fusion | flops 2521497600 | bytes 12974080 | tf_op jit(solution)/shard_map/rd,cdh->rch/dot_general | solution.py:63
  71.2 0.1 pad_maximum_fusion.1
  71.3 0.6 gather_fusion
  71.9 0.0 copy-start.2
  71.9 0.1 copy.15
  72.0 0.0 copy-start.1
  72.0 0.9 copy-done.2
  72.9 0.6 fusion.27
  73.5 0.0 copy-start.3
  73.5 0.6 fusion.29
  74.1 0.4 copy-done.3
  74.5 0.6 fusion.31
  75.1 0.6 convolution_bitcast_fusion.1
  75.7 0.8 convolution_bitcast_fusion.2
  76.5 0.6 convolution_bitcast_fusion
  77.1 1.6 pad_maximum_fusion
  78.7 0.0 all-reduce.2.cloned.1.call-update
  78.7 101.8 %all-reduce.2.cloned.1.call-done = f32[3,320,640]{2,1,0:T(8,128)} async-done(((f32[3,320,640]{2,1,0:T(8,128)}), f32[3,320,640]{2,1,0:T(8,128)}) %all-reduce.2.cloned.1.call-update) | async-done | bytes 2457616 | tf_op jit(solution)/shard_map/psum | solution.py:76
  180.6 2.4 %fusion.8 = (f32[3,640]{1,0:T(4,128)S(1)}, f32[3,640]{1,0:T(4,128)S(1)}) fusion(bf16[1,320,640]{2,1,0:T(8,128)(2,1)S(1)} %copy-done.3, bf16[1,320,640]{2,1,0:T(8,128)(2,1)S(1)} %copy-done.1, bf16[1,320,640]{2,1,0:T(8,128)(2,1)S(1)} %copy-done.2, f32[3,320,640]{2,1,0:T(8,128)} %all-reduce.2.cloned.1.call-done), kind=kLoop, calls=%fused_computation.11 | loop fusion | flops 4911360 | bytes 3701760 | tf_op jit(solution)/shard_map/reduce_sum | solution.py:75
  183.0 0.1 copy-done
  183.0 0.4 multiply_convert_fusion
  183.4 1.6 fusion.26
  185.0 2.3 %multiply_reduce_fusion.1 = (f32[512]{0:T(512)S(1)}, f32[512,320]{0,1:T(8,128)S(1)}) fusion(bf16[3,320,640]{2,1,0:T(8,128)(2,1)S(1)} %multiply_convert_fusion, f32[512,640]{1,0:T(8,128)} %fusion.26, bf16[512,3,320]{0,2,1:T(8,128)(2,1)S(1)} %bitcast.102), kind=kOutput, calls=%fused_computation.37 | convolution fusion | flops 421723648 | bytes 3115008 | tf_op jit(solution)/shard_map/dot_general | solution.py:47
  187.4 0.1 multiply_convert_fusion.6
  187.5 7.9 %all_to_all.19 = bf16[2,256,320]{1,2,0:T(8,128)(2,1)S(1)} all-to-all(bf16[2,256,320]{1,2,0:T(8,128)(2,1)S(1)} %bitcast.103), channel_id=1, replica_groups=mesh['seq'=16,'head'=2] {'head'}, dimensions={0} | all-to-all | bytes 655360 | tf_op jit(solution)/shard_map/all_to_all | solution.py:81
  195.4 0.9 copy.12
  (12 shorter events, 0.1 us)
Async XLA Ops:
  6.5 174.1 %all-reduce.2.cloned.1.call-start = ((), (), s32[]{:S(2)}) async-start(), calls=%async_computation.1 | async-start | bytes 4915200 | tf_op jit(solution)/shard_map/psum | solution.py:76
  6.5 60.1 %collective-permute-start = (bf16[256,5120]{1,0:T(8,128)(2,1)}, bf16[256,5120]{1,0:T(8,128)(2,1)}, u32[]{:S(2)}, u32[]{:S(2)}) collective-permute-start(bf16[256,5120]{1,0:T(8,128)(2,1)} %param.8), channel_id=1, source_target_pairs={{0,1},{1,0},{2,3},{3,2},{4,5},{5,4},{6,7},{7,6},{8,9},{9,8},{10,11... | collective-permute-start | bytes 7864328 | tf_op jit(solution)/shard_map/ppermute | solution.py:19
  11.7 55.0 %copy-start.4 = (bf16[3,5120,320]{1,2,0:T(8,128)(2,1)S(1)}, bf16[3,5120,320]{1,2,0:T(8,128)(2,1)}, u32[]{:S(2)}) copy-start(bf16[3,5120,320]{1,2,0:T(8,128)(2,1)} %param.9) | copy-start | bytes 29491204
  71.9 1.0 copy-start.2
  72.0 1.5 copy-start.1
  73.5 1.0 copy-start.3
  180.6 2.4 %copy-start = (f32[3,320,640]{2,1,0:T(8,128)S(1)}, f32[3,320,640]{2,1,0:T(8,128)}, u32[]{:S(2)}) copy-start(f32[3,320,640]{2,1,0:T(8,128)} %all-reduce.2.cloned.1.call-done) | copy-start | bytes 7372804
Sparse Core Ops, SparseCore 0:
  78.9 101.6 all-reduce.1
